TPU v7x, 512 devices: a whole 4x4x16 slice. The times are simulated.
512 devices in a mesh: row: 16 (over x, y), col: 32 (over z, core).
Axes of the slice: x: 4, y: 4, z: 16, core: 2. Of those that a mesh axis runs over, the one named last changes fastest.
Arguments:
- positions: float32 [3, 32768], P(None, ('row', 'col')), may hold values from -1 to 96, as said below
- noise: float32 [8, 3, 32768], P(None, None, ('row', 'col')), may hold values from -6 to 6
Outputs:
- basis: float32 [8, 3, 32768], P(None, None, ('row', 'col'))
- residual: float32 [8, 3, 32768], P(None, None, ('row', 'col'))
- coefficients: float32 [3, 8, 8], replicated
Inputs may be any that keep to these rules, and one draw needn't show every extreme that they name: `positions`: bead k lies within 0.77 of each coordinate of its own point of a cubic lattice of spacing 2.2 with 32 by 32 points a layer, distinct beads on distinct points.
All inputs are finite; a program needn't handle non-finite values.
Results may differ from a plain program's by a relative error of at most 0.0003.
Values sent between devices are 32-bit elements; how exact they have to be, the bound alone decides.
A program may use at most 64 MiB of HBM per device.

v0:
```python
import jax
import jax.numpy as jnp
from jax import lax
from jax.sharding import PartitionSpec as P


def pair_tensor(target_pos, source_pos):
    displace = target_pos[:, :, None] - source_pos[:, None, :]
    distance_sq = jnp.sum(displace * displace, axis=0)
    distance = jnp.sqrt(distance_sq)
    safe_distance = jnp.where(distance > 0, distance, 1.0)
    safe_sq = safe_distance * safe_distance
    far_iso = 0.75 / safe_distance * (1.0 + 2.0 / (3.0 * safe_sq))
    far_dir = 0.75 / safe_distance * (1.0 - 2.0 / safe_sq) / safe_sq
    near_iso = 1.0 - 9.0 * distance / 32.0
    near_dir = 3.0 / (32.0 * safe_distance)
    intersecting = distance < 2.0
    iso_part = jnp.where(intersecting, near_iso, far_iso)
    dir_part = jnp.where(intersecting, near_dir, far_dir)
    identity = jnp.eye(3, dtype=displace.dtype)
    return identity[:, :, None, None] * iso_part + dir_part * displace[:, None] * displace[None, :]


def local_gram(left, right):
    return jnp.einsum("kan,jan->kj", left, right, precision=lax.Precision.HIGHEST)


def combine(vectors, matrix):
    return jnp.einsum("kan,kj->jan", vectors, matrix, precision=lax.Precision.HIGHEST)


def lower_inverse(factor):
    return jax.scipy.linalg.solve_triangular(
        factor, jnp.eye(factor.shape[0], dtype=factor.dtype), lower=True
    )


def local(positions, noise):
    local_beads = positions.shape[1]
    total_count = 3.0 * local_beads * lax.axis_size("row") * lax.axis_size("col")
    target_pos = lax.all_gather(positions, "row", axis=1, tiled=True)
    source_pos = lax.all_gather(positions, "col", axis=1, tiled=True)

    def mobility(vectors):
        initial = jnp.zeros((vectors.shape[0], 3, target_pos.shape[1]), jnp.float32)
        source_piece = lax.all_gather(vectors, "col", axis=2, tiled=True)
        piece_width = source_piece.shape[2]
        block_count = 1
        while piece_width % block_count != 0 or piece_width // block_count > 256:
            block_count = block_count + 1
        block_width = piece_width // block_count

        def add_block(block_index, running):
            block_pos = lax.dynamic_slice_in_dim(
                source_pos, block_index * block_width, block_width, 1
            )
            block_vectors = lax.dynamic_slice_in_dim(
                source_piece, block_index * block_width, block_width, 2
            )
            tensor = pair_tensor(target_pos, block_pos)
            return running + jnp.einsum(
                "abts,kbs->kat", tensor, block_vectors, precision=lax.Precision.HIGHEST
            )

        partial_image = lax.fori_loop(0, block_count, add_block, initial)
        summed = lax.psum(partial_image, "row")
        return lax.dynamic_slice_in_dim(summed, lax.axis_index("row") * local_beads, local_beads, 2)

    start_matrix = lax.psum(local_gram(noise, noise), ("row", "col")) / total_count
    start_factor = jnp.linalg.cholesky(start_matrix)
    first = combine(noise, lower_inverse(start_factor).T)
    image = mobility(first)
    alpha_one = lax.psum(local_gram(first, image), ("row", "col")) / total_count
    remainder = image - combine(first, alpha_one)
    residual_matrix = lax.psum(local_gram(remainder, remainder), ("row", "col")) / total_count
    factor_one = jnp.linalg.cholesky(residual_matrix)
    basis = combine(remainder, lower_inverse(factor_one).T)
    image = mobility(basis) - combine(first, factor_one)
    alpha_two = lax.psum(local_gram(basis, image), ("row", "col")) / total_count
    residual = image - combine(basis, alpha_two)
    return (basis, residual, jnp.stack([alpha_one, factor_one, alpha_two]))


def solution(mesh):
    return jax.shard_map(
        local,
        mesh=mesh,
        in_specs=(P(None, ("row", "col")), P(None, None, ("row", "col"))),
        out_specs=(P(None, None, ("row", "col")), P(None, None, ("row", "col")), P()),
        check_vma=False,
    )
```

profile of v0, /device:TPU:1, one launch (start us, length us, event | category | flops | bytes accessed | tf_op | source)
XLA Modules:
  0.0 1041.4 jit_solution(14341036072423276544)
XLA Ops:
  7.2 38.0 %all-gather.1 = f32[32,64,3]{1,2,0:T(4,128)S(1)} all-gather(f32[1,64,3]{1,2,0:T(4,128)} %bitcast.96), channel_id=1, replica_groups=mesh['row'=16,'col'=32] {'col'}, dimensions={0}, use_global_device_ids=true | all-gather | bytes 25344 | tf_op jit(solution)/shard_map/all_gather | solution.py:42
  45.2 18.3 %all-gather = f32[16,64,3]{1,2,0:T(4,128)S(1)} all-gather(f32[1,64,3]{1,2,0:T(4,128)} %bitcast.97), channel_id=1, replica_groups=mesh['row'=16,'col'=32] {'row'}, dimensions={0}, use_global_device_ids=true | all-gather | bytes 13056 | tf_op jit(solution)/shard_map/all_gather | solution.py:41
  63.7 104.2 %psum.42 = f32[8,8]{0,1:T(8,128)S(1)} all-reduce(f32[8,8]{0,1:T(8,128)S(1)} %convolution_bitcast_fusion.5), channel_id=1, replica_groups=mesh['row'=16,'col'=32] {'row','col'}, use_global_device_ids=true, to_apply=%region_0.0 | all-reduce | flops 64 | bytes 512 | tf_op jit(solution)/shard_map/psum | solution.py:69
  171.1 44.3 %all_gather.12 = f32[8,3,2048]{0,1,2:T(4,128)} all-gather(f32[8,3,64]{0,1,2:T(4,128)S(1)} %copy.36), channel_id=1, replica_groups=mesh['row'=16,'col'=32] {'col'}, dimensions={2}, use_global_device_ids=true | all-gather | bytes 202752 | tf_op jit(solution)/shard_map/all_gather | solution.py:46
  215.4 3.3 copy.39
  218.9 120.9 %while.32 = (s32[]{:T(128)}, f32[8,3,1024]{2,0,1:T(8,128)S(1)}, f32[8,3,2048]{2,0,1:T(8,128)S(1)}, f32[3,1024]{1,0:T(4,128)S(1)}, f32[3,2048]{1,0:T(4,128)S(1)},...) while((s32[]{:T(128)}, f32[8,3,1024]{2,0,1:T(8,128)S(1)}, f32[8,3,2048]{2,0,1:T(8,128)S(1)}, ...), condition=%wide.region_5.8_spmd.clone, body=%wide.region_3.7_spmd.clone.sunk | while | flops 242270240 | bytes 19134656 | solution.py:65
  219.4 2.0 multiply_select_fusion.4
  221.4 2.1 subtract_multiply_fusion.4
  223.5 10.5 %fusion.87 = f32[8,3,1024]{2,0,1:T(8,128)S(1)} fusion(f32[3,1024,256]{2,1,0:T(8,128)} %get-tuple-element.423, f32[3,1024,256]{2,1,0:T(8,128)S(1)} %get-tuple-element.424, f32[1024,256]{1,0:T(8,128)} %get-tuple-element.425, f32[3,3]{1,0:T(4,128)S(1)} %fusion.86, f32[8,3,1024]{2,0,1:T(8,128)S(1)} %get-tuple-element.445, pred[]{:T(512)S(6)} %compare.14, ...), kind=kOutput, calls=%fused_computation.13.clone.1 | convolution fusion | flops 233619456 | bytes 7563269 | tf_op jit(solution)/shard_map/while/body/eval_jaxpr/abts,kbs->kat/dot_general | solution.py:61
  234.5 2.0 multiply_select_fusion.4
  236.5 2.1 subtract_multiply_fusion.4
  238.7 10.5 %fusion.87 = f32[8,3,1024]{2,0,1:T(8,128)S(1)} fusion(f32[3,1024,256]{2,1,0:T(8,128)} %get-tuple-element.423, f32[3,1024,256]{2,1,0:T(8,128)S(1)} %get-tuple-element.424, f32[1024,256]{1,0:T(8,128)} %get-tuple-element.425, f32[3,3]{1,0:T(4,128)S(1)} %fusion.86, f32[8,3,1024]{2,0,1:T(8,128)S(1)} %get-tuple-element.445, pred[]{:T(512)S(6)} %compare.14, ...), kind=kOutput, calls=%fused_computation.13.clone.1 | convolution fusion | flops 233619456 | bytes 7563269 | tf_op jit(solution)/shard_map/while/body/eval_jaxpr/abts,kbs->kat/dot_general | solution.py:61
  249.6 2.0 multiply_select_fusion.4
  251.6 2.1 subtract_multiply_fusion.4
  253.8 10.5 %fusion.87 = f32[8,3,1024]{2,0,1:T(8,128)S(1)} fusion(f32[3,1024,256]{2,1,0:T(8,128)} %get-tuple-element.423, f32[3,1024,256]{2,1,0:T(8,128)S(1)} %get-tuple-element.424, f32[1024,256]{1,0:T(8,128)} %get-tuple-element.425, f32[3,3]{1,0:T(4,128)S(1)} %fusion.86, f32[8,3,1024]{2,0,1:T(8,128)S(1)} %get-tuple-element.445, pred[]{:T(512)S(6)} %compare.14, ...), kind=kOutput, calls=%fused_computation.13.clone.1 | convolution fusion | flops 233619456 | bytes 7563269 | tf_op jit(solution)/shard_map/while/body/eval_jaxpr/abts,kbs->kat/dot_general | solution.py:61
  264.8 2.0 multiply_select_fusion.4
  266.8 2.1 subtract_multiply_fusion.4
  268.9 10.5 %fusion.87 = f32[8,3,1024]{2,0,1:T(8,128)S(1)} fusion(f32[3,1024,256]{2,1,0:T(8,128)} %get-tuple-element.423, f32[3,1024,256]{2,1,0:T(8,128)S(1)} %get-tuple-element.424, f32[1024,256]{1,0:T(8,128)} %get-tuple-element.425, f32[3,3]{1,0:T(4,128)S(1)} %fusion.86, f32[8,3,1024]{2,0,1:T(8,128)S(1)} %get-tuple-element.445, pred[]{:T(512)S(6)} %compare.14, ...), kind=kOutput, calls=%fused_computation.13.clone.1 | convolution fusion | flops 233619456 | bytes 7563269 | tf_op jit(solution)/shard_map/while/body/eval_jaxpr/abts,kbs->kat/dot_general | solution.py:61
  279.9 2.0 multiply_select_fusion.4
  281.9 2.1 subtract_multiply_fusion.4
  284.0 10.5 %fusion.87 = f32[8,3,1024]{2,0,1:T(8,128)S(1)} fusion(f32[3,1024,256]{2,1,0:T(8,128)} %get-tuple-element.423, f32[3,1024,256]{2,1,0:T(8,128)S(1)} %get-tuple-element.424, f32[1024,256]{1,0:T(8,128)} %get-tuple-element.425, f32[3,3]{1,0:T(4,128)S(1)} %fusion.86, f32[8,3,1024]{2,0,1:T(8,128)S(1)} %get-tuple-element.445, pred[]{:T(512)S(6)} %compare.14, ...), kind=kOutput, calls=%fused_computation.13.clone.1 | convolution fusion | flops 233619456 | bytes 7563269 | tf_op jit(solution)/shard_map/while/body/eval_jaxpr/abts,kbs->kat/dot_general | solution.py:61
  295.0 2.0 multiply_select_fusion.4
  297.0 2.1 subtract_multiply_fusion.4
  299.1 10.5 %fusion.87 = f32[8,3,1024]{2,0,1:T(8,128)S(1)} fusion(f32[3,1024,256]{2,1,0:T(8,128)} %get-tuple-element.423, f32[3,1024,256]{2,1,0:T(8,128)S(1)} %get-tuple-element.424, f32[1024,256]{1,0:T(8,128)} %get-tuple-element.425, f32[3,3]{1,0:T(4,128)S(1)} %fusion.86, f32[8,3,1024]{2,0,1:T(8,128)S(1)} %get-tuple-element.445, pred[]{:T(512)S(6)} %compare.14, ...), kind=kOutput, calls=%fused_computation.13.clone.1 | convolution fusion | flops 233619456 | bytes 7563269 | tf_op jit(solution)/shard_map/while/body/eval_jaxpr/abts,kbs->kat/dot_general | solution.py:61
  310.1 2.0 multiply_select_fusion.4
  312.1 2.1 subtract_multiply_fusion.4
  314.2 10.5 %fusion.87 = f32[8,3,1024]{2,0,1:T(8,128)S(1)} fusion(f32[3,1024,256]{2,1,0:T(8,128)} %get-tuple-element.423, f32[3,1024,256]{2,1,0:T(8,128)S(1)} %get-tuple-element.424, f32[1024,256]{1,0:T(8,128)} %get-tuple-element.425, f32[3,3]{1,0:T(4,128)S(1)} %fusion.86, f32[8,3,1024]{2,0,1:T(8,128)S(1)} %get-tuple-element.445, pred[]{:T(512)S(6)} %compare.14, ...), kind=kOutput, calls=%fused_computation.13.clone.1 | convolution fusion | flops 233619456 | bytes 7563269 | tf_op jit(solution)/shard_map/while/body/eval_jaxpr/abts,kbs->kat/dot_general | solution.py:61
  325.2 2.0 multiply_select_fusion.4
  327.2 2.1 subtract_multiply_fusion.4
  329.4 10.5 %fusion.87 = f32[8,3,1024]{2,0,1:T(8,128)S(1)} fusion(f32[3,1024,256]{2,1,0:T(8,128)} %get-tuple-element.423, f32[3,1024,256]{2,1,0:T(8,128)S(1)} %get-tuple-element.424, f32[1024,256]{1,0:T(8,128)} %get-tuple-element.425, f32[3,3]{1,0:T(4,128)S(1)} %fusion.86, f32[8,3,1024]{2,0,1:T(8,128)S(1)} %get-tuple-element.445, pred[]{:T(512)S(6)} %compare.14, ...), kind=kOutput, calls=%fused_computation.13.clone.1 | convolution fusion | flops 233619456 | bytes 7563269 | tf_op jit(solution)/shard_map/while/body/eval_jaxpr/abts,kbs->kat/dot_general | solution.py:61
  340.6 103.5 %all-reduce.3.cloned.1.call-done = f32[8,3,1024]{2,0,1:T(8,128)} async-done(((f32[8,3,1024]{2,0,1:T(8,128)}), f32[8,3,1024]{2,0,1:T(8,128)}) %all-reduce.3.cloned.1.call-update) | async-done | bytes 98320 | tf_op jit(solution)/shard_map/psum | solution.py:66
  444.0 0.9 convolution_bitcast_fusion.3
  444.9 104.2 %psum.44 = f32[8,8]{0,1:T(8,128)S(1)} all-reduce(f32[8,8]{0,1:T(8,128)S(1)} %convolution_bitcast_fusion.3), channel_id=1, replica_groups=mesh['row'=16,'col'=32] {'row','col'}, use_global_device_ids=true, to_apply=%region_7.10 | all-reduce | flops 64 | bytes 512 | tf_op jit(solution)/shard_map/psum | solution.py:73
  550.1 100.2 %psum.45 = f32[8,8]{0,1:T(8,128)S(1)} all-reduce(f32[8,8]{0,1:T(8,128)S(1)} %convolution_bitcast_fusion.2), channel_id=1, replica_groups=mesh['row'=16,'col'=32] {'row','col'}, use_global_device_ids=true, to_apply=%region_8.11 | all-reduce | flops 64 | bytes 512 | tf_op jit(solution)/shard_map/psum | solution.py:75
  653.5 43.3 %all_gather.15 = f32[8,3,2048]{0,1,2:T(4,128)} all-gather(f32[8,3,64]{0,1,2:T(4,128)S(1)} %copy.44), channel_id=1, replica_groups=mesh['row'=16,'col'=32] {'col'}, dimensions={2}, use_global_device_ids=true | all-gather | bytes 202752 | tf_op jit(solution)/shard_map/all_gather | solution.py:46
  696.8 3.3 copy.45
  700.1 120.9 %while.33 = (s32[]{:T(128)}, f32[8,3,1024]{2,0,1:T(8,128)S(1)}, f32[8,3,2048]{2,0,1:T(8,128)S(1)}, f32[3,1024]{1,0:T(4,128)S(1)}, f32[3,2048]{1,0:T(4,128)S(1)},...) while((s32[]{:T(128)}, f32[8,3,1024]{2,0,1:T(8,128)S(1)}, f32[8,3,2048]{2,0,1:T(8,128)S(1)}, ...), condition=%wide.region_11.14_spmd.clone, body=%wide.region_9.13_spmd.clone.sunk | while | flops 242270240 | bytes 19134656 | solution.py:65
  700.6 2.0 multiply_select_fusion.5
  702.6 2.1 subtract_multiply_fusion.5
  704.8 10.5 %fusion.91 = f32[8,3,1024]{2,0,1:T(8,128)S(1)} fusion(f32[3,1024,256]{2,1,0:T(8,128)} %get-tuple-element.432, f32[3,1024,256]{2,1,0:T(8,128)S(1)} %get-tuple-element.433, f32[1024,256]{1,0:T(8,128)} %get-tuple-element.434, f32[3,3]{1,0:T(4,128)S(1)} %fusion.90, f32[8,3,1024]{2,0,1:T(8,128)S(1)} %get-tuple-element.472, pred[]{:T(512)S(6)} %compare.15, ...), kind=kOutput, calls=%fused_computation.37.clone.1 | convolution fusion | flops 233619456 | bytes 7563269 | tf_op jit(solution)/shard_map/while/body/eval_jaxpr/abts,kbs->kat/dot_general | solution.py:61
  715.8 2.0 multiply_select_fusion.5
  717.8 2.1 subtract_multiply_fusion.5
  719.9 10.5 %fusion.91 = f32[8,3,1024]{2,0,1:T(8,128)S(1)} fusion(f32[3,1024,256]{2,1,0:T(8,128)} %get-tuple-element.432, f32[3,1024,256]{2,1,0:T(8,128)S(1)} %get-tuple-element.433, f32[1024,256]{1,0:T(8,128)} %get-tuple-element.434, f32[3,3]{1,0:T(4,128)S(1)} %fusion.90, f32[8,3,1024]{2,0,1:T(8,128)S(1)} %get-tuple-element.472, pred[]{:T(512)S(6)} %compare.15, ...), kind=kOutput, calls=%fused_computation.37.clone.1 | convolution fusion | flops 233619456 | bytes 7563269 | tf_op jit(solution)/shard_map/while/body/eval_jaxpr/abts,kbs->kat/dot_general | solution.py:61
  730.9 2.0 multiply_select_fusion.5
  732.9 2.1 subtract_multiply_fusion.5
  735.0 10.5 %fusion.91 = f32[8,3,1024]{2,0,1:T(8,128)S(1)} fusion(f32[3,1024,256]{2,1,0:T(8,128)} %get-tuple-element.432, f32[3,1024,256]{2,1,0:T(8,128)S(1)} %get-tuple-element.433, f32[1024,256]{1,0:T(8,128)} %get-tuple-element.434, f32[3,3]{1,0:T(4,128)S(1)} %fusion.90, f32[8,3,1024]{2,0,1:T(8,128)S(1)} %get-tuple-element.472, pred[]{:T(512)S(6)} %compare.15, ...), kind=kOutput, calls=%fused_computation.37.clone.1 | convolution fusion | flops 233619456 | bytes 7563269 | tf_op jit(solution)/shard_map/while/body/eval_jaxpr/abts,kbs->kat/dot_general | solution.py:61
  746.0 2.0 multiply_select_fusion.5
  748.0 2.1 subtract_multiply_fusion.5
  750.1 10.5 %fusion.91 = f32[8,3,1024]{2,0,1:T(8,128)S(1)} fusion(f32[3,1024,256]{2,1,0:T(8,128)} %get-tuple-element.432, f32[3,1024,256]{2,1,0:T(8,128)S(1)} %get-tuple-element.433, f32[1024,256]{1,0:T(8,128)} %get-tuple-element.434, f32[3,3]{1,0:T(4,128)S(1)} %fusion.90, f32[8,3,1024]{2,0,1:T(8,128)S(1)} %get-tuple-element.472, pred[]{:T(512)S(6)} %compare.15, ...), kind=kOutput, calls=%fused_computation.37.clone.1 | convolution fusion | flops 233619456 | bytes 7563269 | tf_op jit(solution)/shard_map/while/body/eval_jaxpr/abts,kbs->kat/dot_general | solution.py:61
  761.1 2.0 multiply_select_fusion.5
  763.1 2.1 subtract_multiply_fusion.5
  765.2 10.5 %fusion.91 = f32[8,3,1024]{2,0,1:T(8,128)S(1)} fusion(f32[3,1024,256]{2,1,0:T(8,128)} %get-tuple-element.432, f32[3,1024,256]{2,1,0:T(8,128)S(1)} %get-tuple-element.433, f32[1024,256]{1,0:T(8,128)} %get-tuple-element.434, f32[3,3]{1,0:T(4,128)S(1)} %fusion.90, f32[8,3,1024]{2,0,1:T(8,128)S(1)} %get-tuple-element.472, pred[]{:T(512)S(6)} %compare.15, ...), kind=kOutput, calls=%fused_computation.37.clone.1 | convolution fusion | flops 233619456 | bytes 7563269 | tf_op jit(solution)/shard_map/while/body/eval_jaxpr/abts,kbs->kat/dot_general | solution.py:61
  776.2 2.0 multiply_select_fusion.5
  778.2 2.1 subtract_multiply_fusion.5
  780.4 10.5 %fusion.91 = f32[8,3,1024]{2,0,1:T(8,128)S(1)} fusion(f32[3,1024,256]{2,1,0:T(8,128)} %get-tuple-element.432, f32[3,1024,256]{2,1,0:T(8,128)S(1)} %get-tuple-element.433, f32[1024,256]{1,0:T(8,128)} %get-tuple-element.434, f32[3,3]{1,0:T(4,128)S(1)} %fusion.90, f32[8,3,1024]{2,0,1:T(8,128)S(1)} %get-tuple-element.472, pred[]{:T(512)S(6)} %compare.15, ...), kind=kOutput, calls=%fused_computation.37.clone.1 | convolution fusion | flops 233619456 | bytes 7563269 | tf_op jit(solution)/shard_map/while/body/eval_jaxpr/abts,kbs->kat/dot_general | solution.py:61
  791.3 2.0 multiply_select_fusion.5
  793.3 2.1 subtract_multiply_fusion.5
  795.5 10.5 %fusion.91 = f32[8,3,1024]{2,0,1:T(8,128)S(1)} fusion(f32[3,1024,256]{2,1,0:T(8,128)} %get-tuple-element.432, f32[3,1024,256]{2,1,0:T(8,128)S(1)} %get-tuple-element.433, f32[1024,256]{1,0:T(8,128)} %get-tuple-element.434, f32[3,3]{1,0:T(4,128)S(1)} %fusion.90, f32[8,3,1024]{2,0,1:T(8,128)S(1)} %get-tuple-element.472, pred[]{:T(512)S(6)} %compare.15, ...), kind=kOutput, calls=%fused_computation.37.clone.1 | convolution fusion | flops 233619456 | bytes 7563269 | tf_op jit(solution)/shard_map/while/body/eval_jaxpr/abts,kbs->kat/dot_general | solution.py:61
  806.4 2.0 multiply_select_fusion.5
  808.4 2.1 subtract_multiply_fusion.5
  810.6 10.5 %fusion.91 = f32[8,3,1024]{2,0,1:T(8,128)S(1)} fusion(f32[3,1024,256]{2,1,0:T(8,128)} %get-tuple-element.432, f32[3,1024,256]{2,1,0:T(8,128)S(1)} %get-tuple-element.433, f32[1024,256]{1,0:T(8,128)} %get-tuple-element.434, f32[3,3]{1,0:T(4,128)S(1)} %fusion.90, f32[8,3,1024]{2,0,1:T(8,128)S(1)} %get-tuple-element.472, pred[]{:T(512)S(6)} %compare.15, ...), kind=kOutput, calls=%fused_computation.37.clone.1 | convolution fusion | flops 233619456 | bytes 7563269 | tf_op jit(solution)/shard_map/while/body/eval_jaxpr/abts,kbs->kat/dot_general | solution.py:61
  821.8 105.6 %all-reduce.5.cloned.1.call-done = f32[8,3,1024]{2,0,1:T(8,128)} async-done(((f32[8,3,1024]{2,0,1:T(8,128)}), f32[8,3,1024]{2,0,1:T(8,128)}) %all-reduce.5.cloned.1.call-update) | async-done | bytes 98320 | tf_op jit(solution)/shard_map/psum | solution.py:66
  927.4 1.6 convolution_subtract_fusion.1
  929.1 104.0 %psum.47 = f32[8,8]{0,1:T(8,128)S(1)} all-reduce(f32[8,8]{0,1:T(8,128)S(1)} %convolution_bitcast_fusion), channel_id=1, replica_groups=mesh['row'=16,'col'=32] {'row','col'}, use_global_device_ids=true, to_apply=%region_13.16 | all-reduce | flops 64 | bytes 512 | tf_op jit(solution)/shard_map/psum | solution.py:79
  (98 shorter events, 18.7 us)
Async XLA Ops:
  7.2 56.4 %copy-start = (f32[8,3,64]{2,0,1:T(8,128)S(1)}, f32[8,3,64]{2,0,1:T(8,128)}, u32[]{:S(2)}) copy-start(f32[8,3,64]{2,0,1:T(8,128)} %param.10) | copy-start | bytes 18436
  7.2 436.9 %all-reduce.3.cloned.1.call-start = ((), (), s32[]{:S(2)}) async-start(), calls=%async_computation | async-start | bytes 196608 | tf_op jit(solution)/shard_map/psum | solution.py:66
  339.8 0.6 copy-start.3
  340.5 586.9 %all-reduce.5.cloned.1.call-start = ((), (), s32[]{:S(2)}) async-start(), calls=%async_computation.1 | async-start | bytes 196608 | tf_op jit(solution)/shard_map/psum | solution.py:66
  653.4 379.7 %copy-start.1 = (f32[8,3,64]{2,0,1:T(8,128)}, f32[8,3,64]{2,0,1:T(8,128)S(1)}, u32[]{:S(2)}) copy-start(f32[8,3,64]{2,0,1:T(8,128)S(1)} %fusion.61) | copy-start | bytes 18436
  821.0 0.6 copy-start.2
Sparse Core Ops, SparseCore 0:
  340.6 103.3 all-reduce.2
  821.8 105.5 all-reduce.4
where the time goes:
time: 1040 us
  blocking collectives  556 us (53%)
  waiting for transfers between devices  209 us (20%)
  matrix products  173 us (17%)
  other arithmetic  80.1 us (8%)
  between operations  14.1 us (1%)
    psum x2, waiting for transfers between devices, mobility(): summed = lax.psum(partial_image, 'row')  209 us
    dot_general x16, matrix products, add_block(): jnp.einsum('abts,kbs->kat', tensor, block_vectors, precision=lax.Precisio...  168 us
    psum x1, blocking collectives, local(): lax.psum(local_gram(noise, noise), ('row', 'col')) / total_count  104 us
    psum x1, blocking collectives, local(): alpha_one = lax.psum(local_gram(first, image), ('row', 'col')) / total_count  104 us
    psum x1, blocking collectives, local(): alpha_two = lax.psum(local_gram(basis, image), ('row', 'col')) / total_count  104 us
    psum x1, blocking collectives, local(): lax.psum(local_gram(remainder, remainder), ('row', 'col')) / total_count  100 us
    all_gather x2, blocking collectives, mobility(): source_piece = lax.all_gather(vectors, 'col', axis=2, tiled=True)  87.6 us
    all_gather x1, blocking collectives, local(): source_pos = lax.all_gather(positions, 'col', axis=1, tiled=True)  38 us
  transfers between devices with their start and end apart: 2, of which 2 were waited for; matrix products, arithmetic and copies ran while one was open for 0% of the time, Pallas kernels for 0%

commit v1 on v0

v1 whole, which is shorter than its diff:
```python
import jax
import jax.numpy as jnp
from jax import lax
from jax.experimental import pallas as pl
from jax.experimental.pallas import tpu as pltpu
from jax.sharding import PartitionSpec as P

F32 = jnp.float32
BF16 = jnp.bfloat16
MESH = pl.DeviceIdType.MESH
HIGHEST = lax.Precision.HIGHEST
NT = (((1,), (1,)), ((), ()))
NN = (((1,), (0,)), ((), ()))
TN = (((0,), (0,)), ((), ()))

COLS = 16
PLANE = 32
WIDTH = 64
NCOL = COLS * WIDTH
NPLANE = PLANE * WIDTH
CENTRE = 34.1
CHUNK = 256
BEADS = 32768


def dot(left, right, dims):
    return lax.dot_general(left, right, dims, preferred_element_type=F32)


def exact_dot(left, right, dims):
    return lax.dot_general(left, right, dims, precision=HIGHEST, preferred_element_type=F32)


def split(value):
    high = value.astype(BF16)
    return high, (value - high.astype(F32)).astype(BF16)


def pair_strip(col_pos, plane_pos):
    shift = [c - p for c, p in zip(col_pos, plane_pos)]
    square = jnp.maximum(shift[0] * shift[0] + shift[1] * shift[1] + shift[2] * shift[2], 1e-12)
    inv = lax.rsqrt(square)
    inv2 = inv * inv
    inv3 = inv * inv2
    near = square < 4.0
    iso = jnp.where(near, 1.0 - (9.0 / 32.0) * (square * inv), 0.75 * inv + 0.5 * inv3)
    along = jnp.where(near, (3.0 / 32.0) * inv, inv3 * (0.75 - 1.5 * inv2))
    return [iso] + [along * s for s in shift]


def lower_factor(matrix):
    row = lax.broadcasted_iota(jnp.int32, (8, 8), 0)
    col = lax.broadcasted_iota(jnp.int32, (8, 8), 1)
    left = matrix
    right = jnp.where(row == col, 1.0, 0.0).astype(F32)
    for j in range(8):
        pivot = 1.0 / left[j : j + 1, j : j + 1]
        ratio = jnp.where(row[:, :1] > j, left[:, j : j + 1] * pivot, 0.0)
        left, right = left - ratio * left[j : j + 1, :], right - ratio * right[j : j + 1, :]
    diagonal = jnp.sum(jnp.where(row == col, left, 0.0), axis=1, keepdims=True)
    scale = lax.rsqrt(diagonal)
    scale = scale * (1.5 - 0.5 * diagonal * scale * scale)
    upper = jnp.where(col >= row, left * scale, 0.0)
    return upper, right * scale


def kernel(
    pos_ref, noise_ref, basis_ref, resid_ref, coef_ref,
    col_pos, col_vec, plane_pos, send1, got1, own_y, plane_vec, send2, got2, gram1, gram2, all1, all2,
    wide, col_row, plane_row, xs, ys, high, low, sent, came,
):
    row = lax.axis_index("row")
    col = lax.axis_index("col")
    x, y, z, core = row // 4, row % 4, col // 2, col % 2

    def plane_peer(j):
        dx, dy, dc = j // 8, j // 2 % 4, j % 2
        there = {"row": (x + dx) % 4 * 4 + (y + dy) % 4, "col": z * 2 + (core + dc) % 2}
        back = ((4 - dx) % 4 * 4 + (4 - dy) % 4) * 2 + dc
        return there, back

    def col_peer(t):
        return {"row": row, "col": (z + t) % 16 * 2 + core}, (16 - t) % 16

    def copy(kind, source, target, slot, back, there):
        return pltpu.make_async_remote_copy(
            src_ref=source, dst_ref=target.at[back], send_sem=sent.at[kind, slot], recv_sem=came.at[kind, back],
            device_id=there, device_id_type=MESH,
        )

    def to_plane(kind, source, target):
        def send(j, carry):
            there, back = plane_peer(j)
            copy(kind, source(j), target, j, back, there).start()
            return carry
        lax.fori_loop(1, PLANE, send, 0)

    def to_col(kind, source, target):
        def send(t, carry):
            there, back = col_peer(t)
            copy(kind, source(t), target, t, back, there).start()
            return carry
        lax.fori_loop(1, COLS, send, 0)

    def arrived(kind, source, target, slot):
        here = {"row": row, "col": col}
        pltpu.make_async_remote_copy(
            src_ref=source, dst_ref=target.at[slot], send_sem=sent.at[kind, slot], recv_sem=came.at[kind, slot],
            device_id=here, device_id_type=MESH,
        ).wait_recv()

    def left(kind, source, target, slot):
        here = {"row": row, "col": col}
        pltpu.make_async_remote_copy(
            src_ref=source, dst_ref=target.at[slot], send_sem=sent.at[kind, slot], recv_sem=came.at[kind, slot],
            device_id=here, device_id_type=MESH,
        ).wait_send()

    def wait_all(kind, source, target, count):
        def step(j, carry):
            arrived(kind, source, target, j)
            return carry
        lax.fori_loop(1, count, step, 0)

    barrier = pltpu.get_barrier_semaphore()

    def greet_plane(j, carry):
        there, back = plane_peer(j)
        pl.semaphore_signal(barrier, inc=1, device_id=there, device_id_type=MESH)
        return carry

    def greet_col(t, carry):
        there, back = col_peer(t)
        pl.semaphore_signal(barrier, inc=1, device_id=there, device_id_type=MESH)
        return carry

    lax.fori_loop(1, COLS, greet_col, 0)
    lax.fori_loop(1, PLANE, greet_plane, 0)
    pl.semaphore_wait(barrier, COLS + PLANE - 2)

    to_col(0, lambda t: pos_ref, col_pos)
    to_plane(2, lambda t: pos_ref, plane_pos)
    to_col(1, lambda t: noise_ref, col_vec)
    col_pos[0] = pos_ref[...]
    plane_pos[0] = pos_ref[...]
    col_vec[0] = noise_ref[...]

    wait_all(0, pos_ref, col_pos, COLS)
    wait_all(2, pos_ref, plane_pos, PLANE)

    for i in range(PLANE // 2):
        plane_row[:, 128 * i : 128 * i + 128] = jnp.concatenate([plane_pos[2 * i], plane_pos[2 * i + 1]], axis=1) - CENTRE
    for i in range(COLS // 2):
        col_row[:, 128 * i : 128 * i + 128] = jnp.concatenate([col_pos[2 * i], col_pos[2 * i + 1]], axis=1) - CENTRE
    equal = lax.broadcasted_iota(jnp.int32, (128, 128), 0) == lax.broadcasted_iota(jnp.int32, (128, 128), 1)

    def widen(i, carry):
        lanes = pl.ds(pl.multiple_of(i * 128, 128), 128)
        for a in range(3):
            spread = jnp.sum(jnp.where(equal, col_row[a : a + 1, lanes], 0.0), axis=1, keepdims=True)
            wide[a, lanes, :] = jnp.broadcast_to(spread, (128, 128))
        return carry

    lax.fori_loop(0, NCOL // 128, widen, 0)

    def rows_of(vec, pos):
        along = pos[0:1] * vec[0:8] + pos[1:2] * vec[8:16] + pos[2:3] * vec[16:24]
        return split(jnp.concatenate([vec, along], axis=0))

    def fill(store, vec, lanes, pos):
        top, rest = rows_of(vec, pos)
        store[0:32, lanes] = top
        store[32:64, lanes] = rest

    wait_all(1, noise_ref, col_vec, COLS)
    for i in range(COLS // 2):
        lanes = pl.ds(128 * i, 128)
        fill(xs, jnp.concatenate([col_vec[2 * i], col_vec[2 * i + 1]], axis=1), lanes, col_row[:, lanes])

    def chunk(step, carry):
        at = NPLANE // CHUNK - 1 - step
        lanes = pl.ds(pl.multiple_of(at * CHUNK, CHUNK), CHUNK)
        here = plane_row[:, lanes]
        plane = [jnp.broadcast_to(here[a : a + 1], (16, CHUNK)) for a in range(3)]

        def strip(s, inner):
            for k in range(2):
                rows = pl.ds(pl.multiple_of(s * 32 + k * 16, 16), 16)
                column = [jnp.concatenate([wide[a, rows, :]] * (CHUNK // 128), axis=1) for a in range(3)]
                for n, value in enumerate(pair_strip(column, plane)):
                    top, rest = split(value)
                    high[n, rows, lanes] = top
                    low[n, rows, lanes] = rest
            return inner

        lax.fori_loop(0, NCOL // 32, strip, 0)
        parts = []
        for n in range(4):
            both = dot(xs[...], high[n, :, lanes], NN)
            parts.append(both[0:32] + both[32:64] + dot(xs[0:32, :], low[n, :, lanes], NN))
        image = []
        for a in range(3):
            e = parts[1 + a]
            image.append(
                parts[0][8 * a : 8 * a + 8] + e[24:32]
                - here[0:1] * e[0:8] - here[1:2] * e[8:16] - here[2:3] * e[16:24]
            )
        image = jnp.concatenate(image, axis=0)
        for i in range(CHUNK // WIDTH):
            send1[at * (CHUNK // WIDTH) + i] = image[:, WIDTH * i : WIDTH * i + WIDTH]

        def send(i, inner):
            j = at * (CHUNK // WIDTH) + i

            @pl.when(j > 0)
            def _():
                there, back = plane_peer(j)
                copy(3, send1.at[j], got1, j, back, there).start()
            return inner

        lax.fori_loop(0, CHUNK // WIDTH, send, 0)
        return carry

    lax.fori_loop(0, NPLANE // CHUNK, chunk, 0)

    wait_all(3, send1.at[0], got1, PLANE)
    total = send1[0]
    for j in range(1, PLANE):
        total = total + got1[j]
    own_y[...] = total
    to_plane(4, lambda j: own_y, plane_vec)
    plane_vec[0] = total
    wait_all(4, own_y, plane_vec, PLANE)
    for i in range(PLANE // 2):
        lanes = pl.ds(128 * i, 128)
        fill(ys, jnp.concatenate([plane_vec[2 * i], plane_vec[2 * i + 1]], axis=1), lanes, plane_row[:, lanes])

    def tile(at, carry):
        rows = pl.ds(pl.multiple_of(at * CHUNK, CHUNK), CHUNK)
        here = col_row[:, rows]
        parts = []
        for n in range(4):
            both = dot(ys[...], high[n, rows, :], NT)
            parts.append(both[0:32] + both[32:64] + dot(ys[0:32, :], low[n, rows, :], NT))
        image = []
        for a in range(3):
            e = parts[1 + a]
            image.append(
                parts[0][8 * a : 8 * a + 8] - e[24:32]
                + here[0:1] * e[0:8] + here[1:2] * e[8:16] + here[2:3] * e[16:24]
            )
        image = jnp.concatenate(image, axis=0)
        for i in range(CHUNK // WIDTH):
            send2[at * (CHUNK // WIDTH) + i] = image[:, WIDTH * i : WIDTH * i + WIDTH]

        def send(i, inner):
            t = at * (CHUNK // WIDTH) + i

            @pl.when(t > 0)
            def _():
                there, back = col_peer(t)
                copy(5, send2.at[t], got2, t, back, there).start()
            return inner

        lax.fori_loop(0, CHUNK // WIDTH, send, 0)
        return carry

    lax.fori_loop(0, NCOL // CHUNK, tile, 0)

    wait_all(5, send2.at[0], got2, COLS)
    final = send2[0]
    for t in range(1, COLS):
        final = final + got2[t]

    vec_n, vec_y, vec_z = noise_ref[...], own_y[...], final
    gram = jnp.zeros((24, 24), F32)
    for a in range(3):
        part = slice(8 * a, 8 * a + 8)
        block = jnp.concatenate([vec_n[part], vec_y[part], vec_z[part]], axis=0)
        gram = gram + exact_dot(block, block, NT)
    gram1[...] = gram
    to_plane(6, lambda j: gram1, all1)
    wait_all(6, gram1, all1, PLANE)
    for j in range(1, PLANE):
        gram = gram + all1[j]
    gram2[...] = gram
    to_col(7, lambda j: gram2, all2)
    all2[0] = gram
    wait_all(7, gram2, all2, COLS)
    gram = all2[(16 - z) % 16]
    for t in range(1, COLS):
        gram = gram + all2[(t + 16 - z) % 16]
    gram = gram * (1.0 / (3.0 * BEADS))

    nn, ny, nz = gram[0:8, 0:8], gram[0:8, 8:16], gram[0:8, 16:24]
    yn, yy, yz = gram[8:16, 0:8], gram[8:16, 8:16], gram[8:16, 16:24]
    upper0, inv0 = lower_factor(nn)
    half = exact_dot(inv0, ny, NN)
    alpha1 = exact_dot(half, inv0, NT)
    image_gram = exact_dot(exact_dot(inv0, yy, NN), inv0, NT)
    upper1, inv1 = lower_factor(image_gram - exact_dot(alpha1, alpha1, TN))
    e_t = exact_dot(inv1, inv0, NN)
    f_t = exact_dot(inv1, exact_dot(alpha1, inv0, TN), NN)
    g_t = exact_dot(upper1, inv0, NN)
    y_w = exact_dot(yz, e_t, NT) - exact_dot(yy, f_t, NT) - exact_dot(yn, g_t, NT)
    n_w = exact_dot(nz, e_t, NT) - exact_dot(ny, f_t, NT) - exact_dot(nn, g_t, NT)
    alpha2 = exact_dot(e_t, y_w, NN) - exact_dot(f_t, n_w, NN)
    coef_ref[0] = alpha1
    coef_ref[1] = upper1.T
    coef_ref[2] = alpha2
    for a in range(3):
        part = slice(8 * a, 8 * a + 8)
        base = exact_dot(e_t, vec_y[part], NN) - exact_dot(f_t, vec_n[part], NN)
        image = exact_dot(e_t, vec_z[part], NN) - exact_dot(f_t, vec_y[part], NN) - exact_dot(g_t, vec_n[part], NN)
        basis_ref[:, a, :] = base
        resid_ref[:, a, :] = image - exact_dot(alpha2, base, TN)

    def drain_plane(j, carry):
        left(2, pos_ref, plane_pos, j)
        left(3, send1.at[0], got1, j)
        left(4, own_y, plane_vec, j)
        left(6, gram1, all1, j)
        return carry

    def drain_col(t, carry):
        left(0, pos_ref, col_pos, t)
        left(1, noise_ref, col_vec, t)
        left(5, send2.at[0], got2, t)
        left(7, gram2, all2, t)
        return carry

    lax.fori_loop(1, PLANE, drain_plane, 0)
    lax.fori_loop(1, COLS, drain_col, 0)


def local(positions, noise):
    vmem = pl.BlockSpec(memory_space=pltpu.VMEM)
    rows = noise.transpose(1, 0, 2).reshape(24, WIDTH)
    return pl.pallas_call(
        kernel,
        out_shape=(
            jax.ShapeDtypeStruct((8, 3, WIDTH), F32),
            jax.ShapeDtypeStruct((8, 3, WIDTH), F32),
            jax.ShapeDtypeStruct((3, 8, 8), F32),
        ),
        in_specs=[vmem, vmem],
        out_specs=(vmem, vmem, vmem),
        scratch_shapes=[
            pltpu.VMEM((COLS, 3, WIDTH), F32),
            pltpu.VMEM((COLS, 24, WIDTH), F32),
            pltpu.VMEM((PLANE, 3, WIDTH), F32),
            pltpu.VMEM((PLANE, 24, WIDTH), F32),
            pltpu.VMEM((PLANE, 24, WIDTH), F32),
            pltpu.VMEM((24, WIDTH), F32),
            pltpu.VMEM((PLANE, 24, WIDTH), F32),
            pltpu.VMEM((COLS, 24, WIDTH), F32),
            pltpu.VMEM((COLS, 24, WIDTH), F32),
            pltpu.VMEM((24, 24), F32),
            pltpu.VMEM((24, 24), F32),
            pltpu.VMEM((PLANE, 24, 24), F32),
            pltpu.VMEM((COLS, 24, 24), F32),
            pltpu.VMEM((3, NCOL, 128), F32),
            pltpu.VMEM((3, NCOL), F32),
            pltpu.VMEM((3, NPLANE), F32),
            pltpu.VMEM((64, NCOL), BF16),
            pltpu.VMEM((64, NPLANE), BF16),
            pltpu.VMEM((4, NCOL, NPLANE), BF16),
            pltpu.VMEM((4, NCOL, NPLANE), BF16),
            pltpu.SemaphoreType.DMA((8, PLANE)),
            pltpu.SemaphoreType.DMA((8, PLANE)),
        ],
        compiler_params=pltpu.CompilerParams(
            collective_id=0, has_side_effects=True, vmem_limit_bytes=60 * 1024 * 1024
        ),
    )(positions, rows)


def solution(mesh):
    return jax.shard_map(
        local,
        mesh=mesh,
        in_specs=(P(None, ("row", "col")), P(None, None, ("row", "col"))),
        out_specs=(P(None, None, ("row", "col")), P(None, None, ("row", "col")), P()),
        check_vma=False,
    )
```

time: 1040 us -> 115 us (0.11)
  blocking collectives: 556 us -> 0 us
  waiting for transfers between devices: 209 us -> 0 us
  matrix products: 173 us -> 0 us
  Pallas kernels: 0 us -> 110 us
  other arithmetic: 80.1 us -> 0 us
  between operations: 14.1 us -> 0.65 us
    psum x4 -> x0, blocking collectives: 413 us -> none  [the longest x1 104 us: local(): lax.psum(local_gram(noise, noise), ('row', 'col')) / total_count]
    psum x2 -> x0, waiting for transfers between devices: 209 us -> none  [mobility(): summed = lax.psum(partial_image, 'row')]
    dot_general x25 -> x0, matrix products: 172 us -> none  [the longest x16 168 us: add_block(): jnp.einsum('abts,kbs->kat', tensor, block_vectors, precision=lax.Precisio...]
    all_gather x4 -> x0, blocking collectives: 144 us -> none  [the longest x2 87.6 us: mobility(): source_piece = lax.all_gather(vectors, 'col', axis=2, tiled=True)]
    pallas_call x0 -> x1, Pallas kernels: none -> 110 us  [local(): pl.pallas_call(kernel, out_shape=(jax.ShapeDtypeStruct((8, 3, WIDTH), F32...]
    mul x16 -> x0, other arithmetic: 34.2 us -> none  [pair_tensor(): dir_part * displace[:, None] * displace[None, :]]
    select_n x16 -> x0, other arithmetic: 32 us -> none  [pair_tensor(): iso_part = jnp.where(intersecting, near_iso, far_iso)]
  transfers between devices with their start and end apart: 2 -> 0, of which waited for: 2 -> 0; matrix products, arithmetic and copies ran while one was open for 0% -> 0% of each run, Pallas kernels for 0% -> 0%
where the time goes in v1:
time: 115 us; the launch traced here: 114 us
  Pallas kernels  110 us (96%)
  local copies, waits for them, and re-layouts  2.64 us (2%)
    pallas_call x1, Pallas kernels, local(): pl.pallas_call(kernel, out_shape=(jax.ShapeDtypeStruct((8, 3, WIDTH), F32...  110 us

profile of v1, /device:TPU:1, one launch (start us, length us, event | category | flops | bytes accessed | tf_op | source)
XLA Modules:
  0.0 113.7 jit_solution(10299532230816750172)
XLA Ops:
  0.6 110.4 %shard_map.49 = (f32[8,3,64]{2,1,0:T(4,128)}, f32[8,3,64]{2,1,0:T(4,128)}, f32[3,8,8]{2,1,0:T(8,128)}) custom-call(f32[3,64]{1,0:T(4,128)} %pos_ref.1, f32[24,64]{1,0:T(8,128)} %bitcast.3), custom_call_target="tpu_custom_call" | custom-call | tf_op jit(solution)/shard_map/pallas_call | solution.py:339
  111.1 0.0 copy-start
  111.1 1.3 %copy.5 = f32[8,3,64]{2,0,1:T(8,128)} copy(f32[8,3,64]{2,1,0:T(4,128)} %get-tuple-element.3) | data formatting | bytes 12288 | tf_op jit(solution)/shard_map/pallas_call | solution.py:339
  112.4 0.0 copy-done
  112.4 0.0 copy-start.1
  112.4 0.6 copy.6
  113.0 0.1 copy-done.1
  113.1 0.6 copy.8
Async XLA Ops:
  111.1 1.3 %copy-start = (f32[8,3,64]{2,1,0:T(4,128)S(1)}, f32[8,3,64]{2,1,0:T(4,128)}, u32[]{:S(2)}) copy-start(f32[8,3,64]{2,1,0:T(4,128)} %get-tuple-element.4) | copy-start | bytes 18436
  112.4 0.7 copy-start.1

commit v2 on v1

v2 whole, which is shorter than its diff:
```python
import jax
import jax.numpy as jnp
from jax import lax
from jax.experimental import pallas as pl
from jax.experimental.pallas import tpu as pltpu
from jax.sharding import PartitionSpec as P

F32 = jnp.float32
BF16 = jnp.bfloat16
MESH = pl.DeviceIdType.MESH
HIGHEST = lax.Precision.HIGHEST
NT = (((1,), (1,)), ((), ()))
NN = (((1,), (0,)), ((), ()))
TN = (((0,), (0,)), ((), ()))

COLS = 16
PLANE = 32
WIDTH = 64
NCOL = COLS * WIDTH
NPLANE = PLANE * WIDTH
CENTRE = 34.1
CHUNK = 256
BEADS = 32768


def dot(left, right, dims):
    return lax.dot_general(left, right, dims, preferred_element_type=F32)


def exact_dot(left, right, dims):
    return lax.dot_general(left, right, dims, precision=HIGHEST, preferred_element_type=F32)


def split(value):
    high = value.astype(BF16)
    return high, (value - high.astype(F32)).astype(BF16)


def pair_strip(col_pos, plane_pos):
    shift = [c - p for c, p in zip(col_pos, plane_pos)]
    square = jnp.maximum(shift[0] * shift[0] + shift[1] * shift[1] + shift[2] * shift[2], 1e-12)
    inv = lax.rsqrt(square)
    inv2 = inv * inv
    inv3 = inv * inv2
    near = square < 4.0
    iso = jnp.where(near, 1.0 - (9.0 / 32.0) * (square * inv), 0.75 * inv + 0.5 * inv3)
    along = jnp.where(near, (3.0 / 32.0) * inv, inv3 * (0.75 - 1.5 * inv2))
    return [iso] + [along * s for s in shift]


def lower_factor(matrix):
    row = lax.broadcasted_iota(jnp.int32, (8, 8), 0)
    col = lax.broadcasted_iota(jnp.int32, (8, 8), 1)
    left = matrix
    right = jnp.where(row == col, 1.0, 0.0).astype(F32)
    for j in range(8):
        pivot = 1.0 / left[j : j + 1, j : j + 1]
        ratio = jnp.where(row[:, :1] > j, left[:, j : j + 1] * pivot, 0.0)
        left, right = left - ratio * left[j : j + 1, :], right - ratio * right[j : j + 1, :]
    diagonal = jnp.sum(jnp.where(row == col, left, 0.0), axis=1, keepdims=True)
    scale = lax.rsqrt(diagonal)
    scale = scale * (1.5 - 0.5 * diagonal * scale * scale)
    upper = jnp.where(col >= row, left * scale, 0.0)
    return upper, right * scale


def kernel(
    pos_ref, noise_ref, basis_ref, resid_ref, coef_ref,
    col_pos, col_vec, plane_pos, send1, got1, own_y, plane_vec, send2, got2, col_y,
    gram1, gram2, all1, all2, cross1, cross2, all3, all4,
    wide, col_row, plane_row, xs, ys, pair, image2, sent, came,
):
    row = lax.axis_index("row")
    col = lax.axis_index("col")
    x, y, z, core = row >> 2, row & 3, col >> 1, col & 1
    here = (row, col)

    def plane_peer(j):
        dx, dy, dc = j >> 3, (j >> 1) & 3, j & 1
        there = (((x + dx) & 3) * 4 + ((y + dy) & 3), z * 2 + (core ^ dc))
        back = ((((4 - dx) & 3) * 4 + ((4 - dy) & 3)) << 1) + dc
        return there, back

    def col_peer(t):
        return (row, ((z + t) & 15) * 2 + core), (16 - t) & 15

    def near(target):
        return [(target, 1, 4), (target, 12, 4), (target, 5, 4), (target, 9, 3)]

    lands = near(col_pos) + near(col_vec) + [
        (plane_pos, 1, PLANE - 1),
        (got1, 1, PLANE - 1),
        (plane_vec, 1, PLANE - 1),
        (col_y, 1, COLS - 1),
        (got2, 1, COLS - 1),
        (all1, 1, PLANE - 1),
        (all2, 1, COLS - 1),
        (all3, 1, PLANE - 1),
        (all4, 1, COLS - 1),
    ]
    POS, VEC, PLACE, SUM1, IMAGE, COLY, SUM2, GRAM1, GRAM2, CROSS1, CROSS2 = 0, 4, 8, 9, 10, 11, 12, 13, 14, 15, 16

    def copy(kind, source, target, there):
        return pltpu.make_async_remote_copy(
            src_ref=source, dst_ref=target, send_sem=sent.at[kind], recv_sem=came.at[kind],
            device_id=there, device_id_type=MESH,
        )

    def whole(kind):
        target, first, count = lands[kind]
        block = target.at[pl.ds(first, count)]
        return copy(kind, block, block, here)

    def wait(*kinds):
        for kind in kinds:
            whole(kind).wait_recv()

    def to_plane(kind, source):
        for j in range(1, PLANE):
            there, back = plane_peer(j)
            copy(kind, source, lands[kind][0].at[back], there).start()

    def to_col(kind, source):
        for t in range(1, COLS):
            there, back = col_peer(t)
            copy(kind, source, lands[kind][0].at[back], there).start()

    def to_near(kind, source):
        for d in range(1, 5):
            for side, t in ((0, 16 - d), (1, d)):
                there, back = col_peer(t)
                copy(kind + side, source, lands[kind][0].at[back], there).start()

    def relay(kind):
        target = lands[kind][0]
        wait(kind)
        copy(kind + 2, target.at[pl.ds(1, 4)], target.at[pl.ds(5, 4)], col_peer(12)[0]).start()
        wait(kind + 1)
        copy(kind + 3, target.at[pl.ds(13, 3)], target.at[pl.ds(9, 3)], col_peer(4)[0]).start()

    def each(count, step, start=0):
        def body(j, carry):
            step(j)
            return carry
        lax.fori_loop(start, count, body, 0)

    barrier = pltpu.get_barrier_semaphore()
    for peer, slots in ((plane_peer, range(1, PLANE)), (col_peer, (1, 2, 3, 4, 12, 13, 14, 15))):
        for j in slots:
            pl.semaphore_signal(barrier, inc=1, device_id=peer(j)[0], device_id_type=MESH)
    pl.semaphore_wait(barrier, PLANE + 7)

    to_near(POS, pos_ref)
    to_plane(PLACE, pos_ref)
    to_near(VEC, noise_ref)
    col_pos[0] = pos_ref[...]
    plane_pos[0] = pos_ref[...]
    col_vec[0] = noise_ref[...]

    relay(POS)
    wait(PLACE)
    for i in range(PLANE // 2):
        plane_row[:, 128 * i : 128 * i + 128] = jnp.concatenate([plane_pos[2 * i], plane_pos[2 * i + 1]], axis=1) - CENTRE
    equal = lax.broadcasted_iota(jnp.int32, (128, 128), 0) == lax.broadcasted_iota(jnp.int32, (128, 128), 1)

    def lanes_of(at):
        return pl.ds(pl.multiple_of(at * CHUNK, CHUNK), CHUNK)

    def plane_of(at):
        here = plane_row[:, lanes_of(at)]
        return [jnp.broadcast_to(here[a : a + 1], (16, CHUNK)) for a in range(3)]

    def build(i, at, plane):
        for k in range(8):
            rows = pl.ds(pl.multiple_of(i * 128 + k * 16, 16), 16)
            column = [jnp.concatenate([wide[a, rows, :]] * (CHUNK // 128), axis=1) for a in range(3)]
            for n, value in enumerate(pair_strip(column, plane)):
                top, rest = split(value)
                pair[2 * n, rows, lanes_of(at)] = top
                pair[2 * n + 1, rows, lanes_of(at)] = rest

    last = NPLANE // CHUNK - 1

    def prepare(i):
        lanes = pl.ds(pl.multiple_of(i * 128, 128), 128)
        both = jnp.concatenate([col_pos[2 * i], col_pos[2 * i + 1]], axis=1) - CENTRE
        col_row[:, lanes] = both
        for a in range(3):
            spread = jnp.sum(jnp.where(equal, both[a : a + 1], 0.0), axis=1, keepdims=True)
            wide[a, lanes, :] = jnp.broadcast_to(spread, (128, 128))

    plane = plane_of(last)

    def first(k):
        i = k + (k >> 1) * 4
        prepare(i)
        build(i, last, plane)

    def second(k):
        prepare(k)
        build(k, last, plane)

    each(4, first)
    wait(POS + 2, POS + 3)
    each(6, second, 2)
    relay(VEC)

    def build_all(at):
        plane = plane_of(at)
        each(8, lambda i: build(i, at, plane))

    build_all(last - 1)

    def fill(store, vec, lanes, pos):
        along = pos[0:1] * vec[0:8] + pos[1:2] * vec[8:16] + pos[2:3] * vec[16:24]
        top, rest = split(jnp.concatenate([vec, along], axis=0))
        store[0:32, lanes] = top
        store[32:64, lanes] = rest

    wait(VEC + 2, VEC + 3)
    for i in range(COLS // 2):
        lanes = pl.ds(128 * i, 128)
        vec = jnp.concatenate([col_vec[2 * i], col_vec[2 * i + 1]], axis=1)
        fill(xs, vec, lanes, col_row[:, lanes])

    def pack(value, lane):
        x, y, z = (value[8 * a : 8 * a + 8, lane : lane + WIDTH] for a in range(3))
        return jnp.concatenate([x, y], axis=1), jnp.concatenate([z, jnp.zeros_like(z)], axis=1)

    def unpack(one, two):
        return jnp.concatenate([
            jnp.concatenate([one[0:8, 0:WIDTH], two[0:8, 0:WIDTH]], axis=1),
            jnp.concatenate([one[0:8, WIDTH:], two[0:8, WIDTH:]], axis=1),
            jnp.concatenate([one[8:16, 0:WIDTH], two[8:16, 0:WIDTH]], axis=1),
        ], axis=0)

    def finish(at):
        here = plane_row[:, lanes_of(at)]
        full = []
        for n in range(4):
            both = dot(xs[...], pair[2 * n, :, lanes_of(at)], NN)
            full.append(both[0:32] + both[32:64] + dot(xs[0:32, :], pair[2 * n + 1, :, lanes_of(at)], NN))
        image = []
        for a in range(3):
            e = full[1 + a]
            image.append(
                full[0][8 * a : 8 * a + 8] + e[24:32]
                - here[0:1] * e[0:8] - here[1:2] * e[8:16] - here[2:3] * e[16:24]
            )
        image = jnp.concatenate(image, axis=0)
        for i in range(CHUNK // WIDTH):
            top, rest = pack(image, WIDTH * i)
            send1[at * (CHUNK // WIDTH) + i, 0:8] = top
            send1[at * (CHUNK // WIDTH) + i, 8:16] = rest

        for i in range(CHUNK // WIDTH):
            j = at * (CHUNK // WIDTH) + i

            @pl.when(j > 0)
            def _():
                there, back = plane_peer(j)
                copy(SUM1, send1.at[j], got1.at[back], there).start()

    finish(last)
    finish(last - 1)

    def chunk(step):
        at = last - step
        build_all(at)
        finish(at)

    each(NPLANE // CHUNK, chunk, 2)

    wait(SUM1)
    total = send1[0]
    for j in range(1, PLANE):
        total = total + got1[j]
    own_y[...] = total
    to_plane(IMAGE, own_y)
    to_col(COLY, own_y)
    plane_vec[0] = total
    col_y[0] = total

    def side(value):
        return jnp.concatenate([value[0:8], value[8:16, 0:WIDTH]], axis=1)

    vec_n = noise_ref[...]
    wide_n = jnp.concatenate([vec_n[0:8], vec_n[8:16], vec_n[16:24]], axis=1)
    wide_y = side(total)
    block = jnp.concatenate([wide_n, wide_y], axis=0)
    gram = exact_dot(block, block, NT)
    gram1[...] = gram
    to_plane(GRAM1, gram1)
    all1[0] = gram

    wait(IMAGE)
    for i in range(PLANE // 2):
        lanes = pl.ds(128 * i, 128)
        fill(ys, unpack(plane_vec[2 * i], plane_vec[2 * i + 1]), lanes, plane_row[:, lanes])

    def tile(at):
        rows = lanes_of(at)
        here = col_row[:, rows]
        full = []
        for n in range(4):
            both = dot(ys[...], pair[2 * n, rows, :], NT)
            full.append(both[0:32] + both[32:64])
        image = []
        for a in range(3):
            e = full[1 + a]
            image.append(
                full[0][8 * a : 8 * a + 8] - e[24:32]
                + here[0:1] * e[0:8] + here[1:2] * e[8:16] + here[2:3] * e[16:24]
            )
        image = jnp.concatenate(image, axis=0)
        image2[:, rows] = image
        for i in range(CHUNK // WIDTH):
            top, rest = pack(image, WIDTH * i)
            send2[at * (CHUNK // WIDTH) + i, 0:8] = top
            send2[at * (CHUNK // WIDTH) + i, 8:16] = rest

        for i in range(CHUNK // WIDTH):
            t = at * (CHUNK // WIDTH) + i

            @pl.when(t > 0)
            def _():
                there, back = col_peer(t)
                copy(SUM2, send2.at[t], got2.at[back], there).start()

    each(NCOL // CHUNK, tile)

    wait(COLY)
    cross = jnp.zeros((8, 8), F32)
    y_rows = jnp.concatenate([unpack(col_y[t], col_y[t + 1]) for t in range(0, COLS, 2)], axis=1)
    for a in range(3):
        part = slice(8 * a, 8 * a + 8)
        cross = cross + exact_dot(y_rows[part], image2[part, :], NT)
    cross1[...] = cross
    to_plane(CROSS1, cross1)
    all3[0] = cross

    wait(GRAM1)
    for j in range(1, PLANE):
        gram = gram + all1[j]
    gram2[...] = gram
    to_col(GRAM2, gram2)
    all2[0] = gram

    wait(CROSS1)
    for j in range(1, PLANE):
        cross = cross + all3[j]
    cross2[...] = cross
    to_col(CROSS2, cross2)
    all4[0] = cross

    def planes(store):
        value = store[(16 - z) % 16]
        for t in range(1, COLS):
            value = value + store[(t + 16 - z) % 16]
        return value * (1.0 / (3.0 * BEADS))

    wait(GRAM2)
    gram = planes(all2)
    nn, ny, yn, yy = gram[0:8, 0:8], gram[0:8, 8:16], gram[8:16, 0:8], gram[8:16, 8:16]
    upper0, inv0 = lower_factor(nn)
    alpha1 = exact_dot(exact_dot(inv0, ny, NN), inv0, NT)
    image_gram = exact_dot(exact_dot(inv0, yy, NN), inv0, NT)
    upper1, inv1 = lower_factor(image_gram - exact_dot(alpha1, alpha1, TN))
    e_t = exact_dot(inv1, inv0, NN)
    f_t = exact_dot(inv1, exact_dot(alpha1, inv0, TN), NN)
    g_t = exact_dot(upper1, inv0, NN)
    y_w = exact_dot(yy, f_t, NT) + exact_dot(yn, g_t, NT)
    n_w = exact_dot(yy, e_t, NT) - exact_dot(ny, f_t, NT) - exact_dot(nn, g_t, NT)
    known = exact_dot(e_t, y_w, NN) + exact_dot(f_t, n_w, NN)
    coef_ref[0] = alpha1
    coef_ref[1] = upper1.T

    base = exact_dot(e_t, wide_y, NN) - exact_dot(f_t, wide_n, NN)
    rest = exact_dot(f_t, wide_y, NN) + exact_dot(g_t, wide_n, NN)

    wait(SUM2)
    final = send2[0]
    for t in range(1, COLS):
        final = final + got2[t]
    image = exact_dot(e_t, side(final), NN) - rest
    for a in range(3):
        basis_ref[8 * a : 8 * a + 8] = base[:, WIDTH * a : WIDTH * a + WIDTH]

    wait(CROSS2)
    alpha2 = exact_dot(e_t, exact_dot(planes(all4), e_t, NT), NN) - known
    coef_ref[2] = alpha2
    residual = image - exact_dot(alpha2, base, TN)
    for a in range(3):
        resid_ref[8 * a : 8 * a + 8] = residual[:, WIDTH * a : WIDTH * a + WIDTH]

    for kind in range(len(lands)):
        whole(kind).wait_send()


def local(positions, noise):
    vmem = pl.BlockSpec(memory_space=pltpu.VMEM)
    rows = noise.transpose(1, 0, 2).reshape(24, WIDTH)
    basis, residual, coefficients = pl.pallas_call(
        kernel,
        out_shape=(
            jax.ShapeDtypeStruct((24, WIDTH), F32),
            jax.ShapeDtypeStruct((24, WIDTH), F32),
            jax.ShapeDtypeStruct((3, 8, 8), F32),
        ),
        in_specs=[vmem, vmem],
        out_specs=(vmem, vmem, vmem),
        scratch_shapes=[
            pltpu.VMEM((COLS, 3, WIDTH), F32),
            pltpu.VMEM((COLS, 24, WIDTH), F32),
            pltpu.VMEM((PLANE, 3, WIDTH), F32),
            pltpu.VMEM((PLANE, 16, 128), F32),
            pltpu.VMEM((PLANE, 16, 128), F32),
            pltpu.VMEM((16, 128), F32),
            pltpu.VMEM((PLANE, 16, 128), F32),
            pltpu.VMEM((COLS, 16, 128), F32),
            pltpu.VMEM((COLS, 16, 128), F32),
            pltpu.VMEM((COLS, 16, 128), F32),
            pltpu.VMEM((16, 16), F32),
            pltpu.VMEM((16, 16), F32),
            pltpu.VMEM((PLANE, 16, 16), F32),
            pltpu.VMEM((COLS, 16, 16), F32),
            pltpu.VMEM((8, 8), F32),
            pltpu.VMEM((8, 8), F32),
            pltpu.VMEM((PLANE, 8, 8), F32),
            pltpu.VMEM((COLS, 8, 8), F32),
            pltpu.VMEM((3, NCOL, 128), F32),
            pltpu.VMEM((3, NCOL), F32),
            pltpu.VMEM((3, NPLANE), F32),
            pltpu.VMEM((64, NCOL), BF16),
            pltpu.VMEM((64, NPLANE), BF16),
            pltpu.VMEM((8, NCOL, NPLANE), BF16),
            pltpu.VMEM((24, NCOL), F32),
            pltpu.SemaphoreType.DMA((17,)),
            pltpu.SemaphoreType.DMA((17,)),
        ],
        compiler_params=pltpu.CompilerParams(
            collective_id=0, has_side_effects=True, vmem_limit_bytes=60 * 1024 * 1024
        ),
    )(positions, rows)

    def back(value):
        return value.reshape(3, 8, WIDTH).transpose(1, 0, 2)

    return back(basis), back(residual), coefficients


def solution(mesh):
    return jax.shard_map(
        local,
        mesh=mesh,
        in_specs=(P(None, ("row", "col")), P(None, None, ("row", "col"))),
        out_specs=(P(None, None, ("row", "col")), P(None, None, ("row", "col")), P()),
        check_vma=False,
    )
```

time: 115 us -> 86.7 us (0.75)
  Pallas kernels: 110 us -> 83 us
    pallas_call x1, Pallas kernels: 110 us -> 83 us  [local(): pl.pallas_call(kernel, out_shape=(jax.ShapeDtypeStruct((24, WIDTH), F32),...]
    pallas_call x2 -> x0, local copies, waits for them, and re-layouts: 1.92 us -> none  [local(): pl.pallas_call(kernel, out_shape=(jax.ShapeDtypeStruct((8, 3, WIDTH), F32...]
    unnamed x5 -> x7, local copies, waits for them, and re-layouts: 0.71 us -> 2.63 us
where the time goes in v2:
time: 86.7 us; the launch traced here: 86.3 us
  Pallas kernels  83 us (96%)
  local copies, waits for them, and re-layouts  2.63 us (3%)
    pallas_call x1, Pallas kernels, local(): pl.pallas_call(kernel, out_shape=(jax.ShapeDtypeStruct((24, WIDTH), F32),...  83 us
    unnamed x7, local copies, waits for them, and re-layouts  2.63 us

profile of v2, /device:TPU:1, one launch (start us, length us, event | category | flops | bytes accessed | tf_op | source)
XLA Modules:
  0.0 86.3 jit_solution(10020122202664382858)
XLA Ops:
  0.6 83.0 %shard_map.49 = (f32[24,64]{1,0:T(8,128)}, f32[24,64]{1,0:T(8,128)}, f32[3,8,8]{2,1,0:T(8,128)}) custom-call(f32[3,64]{1,0:T(4,128)} %pos_ref.1, f32[24,64]{1,0:T(8,128)} %bitcast.9), custom_call_target="tpu_custom_call" | custom-call | tf_op jit(solution)/shard_map/pallas_call | solution.py:403
  83.7 0.0 copy-start.1
  83.7 1.3 %copy.8 = f32[8,3,64]{2,0,1:T(8,128)} copy(f32[8,3,64]{2,0,1:T(8,128)} %bitcast.11) | data formatting | bytes 12288
  85.0 0.0 copy-done.1
  85.0 0.0 copy-start
  85.0 0.6 copy.9
  85.6 0.1 copy-done
  85.7 0.6 copy.10
Async XLA Ops:
  83.7 1.3 %copy-start.1 = (f32[24,64]{1,0:T(8,128)S(1)}, f32[24,64]{1,0:T(8,128)}, u32[]{:S(2)}) copy-start(f32[24,64]{1,0:T(8,128)} %get-tuple-element.7) | copy-start | bytes 18436
  85.0 0.7 copy-start

commit v3 on v2

--- a/solution.py
+++ b/solution.py
@@ -17,10 +17,15 @@
 PLANE = 32
 WIDTH = 64
 NCOL = COLS * WIDTH
+HOPS = (0, 1, 2, 1)
+FAR_FIRST = sorted(range(1, PLANE), key=lambda j: -(2 * (HOPS[j // 8] + HOPS[j // 2 % 4]) + j % 2))
 NPLANE = PLANE * WIDTH
 CENTRE = 34.1
 CHUNK = 256
 BEADS = 32768
+SHRINK = 0.5**0.5
+UNIT = 0.75 * SHRINK
+NEAR = 1.0 / UNIT
 
 
 def dot(left, right, dims):
@@ -42,9 +47,9 @@
     inv = lax.rsqrt(square)
     inv2 = inv * inv
     inv3 = inv * inv2
-    near = square < 4.0
-    iso = jnp.where(near, 1.0 - (9.0 / 32.0) * (square * inv), 0.75 * inv + 0.5 * inv3)
-    along = jnp.where(near, (3.0 / 32.0) * inv, inv3 * (0.75 - 1.5 * inv2))
+    near = square < 2.0
+    iso = jnp.where(near, NEAR - 0.75 * (square * inv), inv + inv3 * (1.0 / 3.0))
+    along = jnp.where(near, 0.25 * inv, inv3 - inv3 * inv2)
     return [iso] + [along * s for s in shift]
 
 
@@ -116,17 +121,17 @@
             whole(kind).wait_recv()
 
     def to_plane(kind, source):
-        for j in range(1, PLANE):
+        for j in FAR_FIRST:
             there, back = plane_peer(j)
             copy(kind, source, lands[kind][0].at[back], there).start()
 
     def to_col(kind, source):
-        for t in range(1, COLS):
+        for t in (8, 7, 9, 6, 10, 5, 11, 4, 12, 3, 13, 2, 14, 1, 15):
             there, back = col_peer(t)
             copy(kind, source, lands[kind][0].at[back], there).start()
 
     def to_near(kind, source):
-        for d in range(1, 5):
+        for d in (4, 3, 2, 1):
             for side, t in ((0, 16 - d), (1, d)):
                 there, back = col_peer(t)
                 copy(kind + side, source, lands[kind][0].at[back], there).start()
@@ -145,7 +150,7 @@
         lax.fori_loop(start, count, body, 0)
 
     barrier = pltpu.get_barrier_semaphore()
-    for peer, slots in ((plane_peer, range(1, PLANE)), (col_peer, (1, 2, 3, 4, 12, 13, 14, 15))):
+    for peer, slots in ((col_peer, (4, 12, 3, 13, 2, 14, 1, 15)), (plane_peer, FAR_FIRST)):
         for j in slots:
             pl.semaphore_signal(barrier, inc=1, device_id=peer(j)[0], device_id_type=MESH)
     pl.semaphore_wait(barrier, PLANE + 7)
@@ -160,7 +165,7 @@
     relay(POS)
     wait(PLACE)
     for i in range(PLANE // 2):
-        plane_row[:, 128 * i : 128 * i + 128] = jnp.concatenate([plane_pos[2 * i], plane_pos[2 * i + 1]], axis=1) - CENTRE
+        plane_row[:, 128 * i : 128 * i + 128] = (jnp.concatenate([plane_pos[2 * i], plane_pos[2 * i + 1]], axis=1) - CENTRE) * SHRINK
     equal = lax.broadcasted_iota(jnp.int32, (128, 128), 0) == lax.broadcasted_iota(jnp.int32, (128, 128), 1)
 
     def lanes_of(at):
@@ -183,7 +188,7 @@
 
     def prepare(i):
         lanes = pl.ds(pl.multiple_of(i * 128, 128), 128)
-        both = jnp.concatenate([col_pos[2 * i], col_pos[2 * i + 1]], axis=1) - CENTRE
+        both = (jnp.concatenate([col_pos[2 * i], col_pos[2 * i + 1]], axis=1) - CENTRE) * SHRINK
         col_row[:, lanes] = both
         for a in range(3):
             spread = jnp.sum(jnp.where(equal, both[a : a + 1], 0.0), axis=1, keepdims=True)
@@ -201,15 +206,15 @@
         build(k, last, plane)
 
     each(4, first)
+    relay(VEC)
     wait(POS + 2, POS + 3)
     each(6, second, 2)
-    relay(VEC)
 
     def build_all(at):
         plane = plane_of(at)
         each(8, lambda i: build(i, at, plane))
 
-    build_all(last - 1)
+    each(4, lambda step: build_all(last - step), 1)
 
     def fill(store, vec, lanes, pos):
         along = pos[0:1] * vec[0:8] + pos[1:2] * vec[8:16] + pos[2:3] * vec[16:24]
@@ -247,7 +252,7 @@
                 full[0][8 * a : 8 * a + 8] + e[24:32]
                 - here[0:1] * e[0:8] - here[1:2] * e[8:16] - here[2:3] * e[16:24]
             )
-        image = jnp.concatenate(image, axis=0)
+        image = jnp.concatenate(image, axis=0) * UNIT
         for i in range(CHUNK // WIDTH):
             top, rest = pack(image, WIDTH * i)
             send1[at * (CHUNK // WIDTH) + i, 0:8] = top
@@ -261,15 +266,14 @@
                 there, back = plane_peer(j)
                 copy(SUM1, send1.at[j], got1.at[back], there).start()
 
-    finish(last)
-    finish(last - 1)
+    each(4, lambda step: finish(last - step))
 
     def chunk(step):
         at = last - step
         build_all(at)
         finish(at)
 
-    each(NPLANE // CHUNK, chunk, 2)
+    each(NPLANE // CHUNK, chunk, 4)
 
     wait(SUM1)
     total = send1[0]
@@ -312,7 +316,7 @@
                 full[0][8 * a : 8 * a + 8] - e[24:32]
                 + here[0:1] * e[0:8] + here[1:2] * e[8:16] + here[2:3] * e[16:24]
             )
-        image = jnp.concatenate(image, axis=0)
+        image = jnp.concatenate(image, axis=0) * UNIT
         image2[:, rows] = image
         for i in range(CHUNK // WIDTH):
             top, rest = pack(image, WIDTH * i)

time: 86.7 us -> 80 us (0.923)
  Pallas kernels: 83 us -> 76.4 us
    pallas_call x1, Pallas kernels: 83 us -> 76.4 us  [local(): pl.pallas_call(kernel, out_shape=(jax.ShapeDtypeStruct((24, WIDTH), F32),...]
where the time goes in v3:
time: 80 us; the launch traced here: 79.7 us
  Pallas kernels  76.4 us (96%)
  local copies, waits for them, and re-layouts  2.63 us (3%)
    pallas_call x1, Pallas kernels, local(): pl.pallas_call(kernel, out_shape=(jax.ShapeDtypeStruct((24, WIDTH), F32),...  76.4 us
    unnamed x7, local copies, waits for them, and re-layouts  2.63 us

profile of v3, /device:TPU:1, one launch (start us, length us, event | category | flops | bytes accessed | tf_op | source)
XLA Modules:
  0.0 79.7 jit_solution(16768636899554253077)
XLA Ops:
  0.6 76.4 %shard_map.49 = (f32[24,64]{1,0:T(8,128)}, f32[24,64]{1,0:T(8,128)}, f32[3,8,8]{2,1,0:T(8,128)}) custom-call(f32[3,64]{1,0:T(4,128)} %pos_ref.1, f32[24,64]{1,0:T(8,128)} %bitcast.9), custom_call_target="tpu_custom_call" | custom-call | tf_op jit(solution)/shard_map/pallas_call | solution.py:407
  77.0 0.0 copy-start.1
  77.0 1.3 %copy.8 = f32[8,3,64]{2,0,1:T(8,128)} copy(f32[8,3,64]{2,0,1:T(8,128)} %bitcast.11) | data formatting | bytes 12288
  78.3 0.0 copy-done.1
  78.3 0.0 copy-start
  78.3 0.6 copy.9
  78.9 0.1 copy-done
  79.1 0.6 copy.10
Async XLA Ops:
  77.0 1.3 %copy-start.1 = (f32[24,64]{1,0:T(8,128)S(1)}, f32[24,64]{1,0:T(8,128)}, u32[]{:S(2)}) copy-start(f32[24,64]{1,0:T(8,128)} %get-tuple-element.7) | copy-start | bytes 18436
  78.3 0.7 copy-start
